TPU v7x, 256 devices: a whole 4x4x8 slice. The times are simulated.
256 devices in a mesh: seq: 64 (over x, z, core), head: 4 (over y).
Axes of the slice: x: 4, y: 4, z: 8, core: 2. Of those that a mesh axis runs over, the one named last changes fastest.
Arguments:
- query_rows: bfloat16 [1, 16384, 2048], P(None, 'seq', 'head'), may hold values from -28 to 28
- key_rows: bfloat16 [1, 16384, 2048], P(None, 'seq', 'head'), may hold values from -4 to 4
- value_rows: bfloat16 [1, 16384, 2048], P(None, 'seq', 'head'), may hold values from -6 to 6
- grad_out: bfloat16 [1, 16384, 2048], P(None, 'seq', 'head'), may hold values from -6 to 6
- rand_blocks: int32 [1, 16, 256, 3], P(None, 'head'), may hold values from 0 to 255, as said below
- global_pos: int32 [128], replicated, may hold values from 0 to 16383, as said below
Outputs:
- attended: bfloat16 [1, 16384, 2048], P(None, 'seq', 'head')
- grad_query: bfloat16 [1, 16384, 2048], P(None, 'seq', 'head')
- grad_key: bfloat16 [1, 16384, 2048], P(None, 'seq', 'head')
- grad_value: bfloat16 [1, 16384, 2048], P(None, 'seq', 'head')
Inputs may be any that keep to these rules, and one draw needn't show every extreme that they name: `rand_blocks`: for each run of 4 query blocks and each run of 4 heads that start at multiples of these counts, taking the one sequence and all 3 picks together, at most 1 picks name a block of any one run of 4 key blocks that starts at a multiple of 4; in each such run of query blocks and heads some run of key blocks is named exactly 1 times. `global_pos`: distinct positions; the first and the last token of the sequence are among them.
All inputs are finite; a program needn't handle non-finite values.
Results may differ from a plain program's by a relative error of at most 0.006.
The roundings to bfloat16 on the way count: a program that leaves them out, or rounds other values in their place, can miss the bound.
Values may be sent and summed in bfloat16 or wider, within the bound.
A program may use at most 64 MiB of HBM per device.

v0:
```python
import jax
import jax.numpy as jnp
from jax import lax
from jax.sharding import PartitionSpec as P

BLOCK = 64


def extended_2(value, sides, width):
    for axis, dim in sides:
        size, length = (lax.axis_size(axis), value.shape[dim])
        up = [(i, (i + 1) % size) for i in range(size - 1)]
        down = [(j, i) for i, j in up]
        last = lax.slice_in_dim(value, length - width, length, axis=dim)
        first = lax.slice_in_dim(value, 0, width, axis=dim)
        before = lax.ppermute(last, axis, up)
        after = lax.ppermute(first, axis, down)
        value = jnp.concatenate([before, value, after], axis=dim)
    return value


def body(query_rows, key_rows, value_rows, grad_out, rand_blocks, global_pos):
    batch_count, tok_local, columns = query_rows.shape
    seq_count = lax.axis_size("seq")
    seq_index = lax.axis_index("seq")
    heads_local = rand_blocks.shape[1]
    total_blocks = rand_blocks.shape[2]
    pick_count = rand_blocks.shape[3]
    head_dim = columns // heads_local
    blocks_local = tok_local // BLOCK
    score_scale = head_dim ** (-0.5)
    slot_count = batch_count * heads_local * blocks_local * pick_count
    capacity = (slot_count + seq_count - 1) // seq_count
    buffer_rows = seq_count * capacity
    f32 = jnp.float32
    bf16 = jnp.bfloat16

    def to_blocks(array):
        return array.reshape(batch_count, blocks_local, BLOCK, heads_local, head_dim).transpose(
            0, 3, 1, 2, 4
        )

    def from_blocks(array):
        return array.transpose(0, 2, 3, 1, 4).reshape(batch_count, tok_local, columns)

    def pair_blocks(array):
        return array.reshape(2, batch_count, blocks_local, BLOCK, heads_local, head_dim).transpose(
            0, 1, 4, 2, 3, 5
        )

    def global_sum(array):
        return lax.psum(array, "seq")

    key_value = jnp.stack([key_rows, value_rows])
    edge_rows = jnp.concatenate([key_value[:, :, :BLOCK], key_value[:, :, -BLOCK:]], axis=2)
    extended = extended_2(edge_rows, (("seq", 2),), BLOCK)
    padded = jnp.concatenate([extended[:, :, :BLOCK], key_value, extended[:, :, -BLOCK:]], axis=2)

    def shifted(start):
        return pair_blocks(padded[:, :, start : start + tok_local])

    window_lists = jnp.concatenate([shifted(0), shifted(BLOCK), shifted(2 * BLOCK)], axis=4)
    my_table = lax.dynamic_slice_in_dim(
        rand_blocks, seq_index * blocks_local, blocks_local, 2
    ).reshape(slot_count)
    holder = my_table // blocks_local
    holder_hot = (holder[:, None] == jnp.arange(seq_count)[None, :]).astype(jnp.int32)
    holder_rank = jnp.sum((jnp.cumsum(holder_hot, axis=0) - 1) * holder_hot, axis=1)
    position = holder * capacity + holder_rank
    requests = rand_blocks.reshape(batch_count, heads_local, seq_count, blocks_local, pick_count)
    requests = requests.transpose(2, 0, 1, 3, 4).reshape(seq_count, slot_count)
    wanted = (requests // blocks_local == seq_index).astype(jnp.int32)
    wanted_rank = jnp.cumsum(wanted, axis=1) - 1
    chosen = wanted[:, None, :] * (
        wanted_rank[:, None, :] == jnp.arange(capacity)[None, :, None]
    ).astype(jnp.int32)
    slot_live = (jnp.sum(chosen, axis=2) > 0).reshape(buffer_rows)
    slot_index = jnp.sum(chosen * jnp.arange(slot_count)[None, None, :], axis=2)
    which_batch = slot_index // (heads_local * blocks_local * pick_count)
    which_head = slot_index // (blocks_local * pick_count) % heads_local
    which_block = jnp.take_along_axis(requests, slot_index, axis=1) % blocks_local
    stacked = key_value.reshape(
        2, batch_count, blocks_local, BLOCK, heads_local, head_dim
    ).transpose(1, 2, 4, 0, 3, 5)
    outgoing = stacked[which_batch, which_block, which_head].reshape(
        buffer_rows, 2, BLOCK, head_dim
    )
    incoming = lax.all_to_all(outgoing, "seq", split_axis=0, concat_axis=0, tiled=True)
    fetched = incoming[position].reshape(
        batch_count, heads_local, blocks_local, pick_count, 2, BLOCK, head_dim
    )
    fetched = fetched.transpose(4, 0, 1, 2, 3, 5, 6).reshape(
        2, batch_count, heads_local, blocks_local, pick_count * BLOCK, head_dim
    )
    local_pos = global_pos - seq_index * tok_local
    pick_hot = (local_pos[:, None] == jnp.arange(tok_local)[None, :]).astype(bf16)
    owned_rows = jnp.einsum("gt,pbtc->pbgc", pick_hot, key_value, preferred_element_type=f32)
    shared = global_sum(owned_rows).astype(bf16)
    globals_count = shared.shape[2]
    global_kv = shared.reshape(2, batch_count, globals_count, heads_local, head_dim).transpose(
        0, 1, 3, 2, 4
    )
    global_kv = jnp.broadcast_to(
        global_kv[:, :, :, None],
        (2, batch_count, heads_local, blocks_local, globals_count, head_dim),
    )
    lists_all = jnp.concatenate([window_lists, fetched, global_kv], axis=4)
    key_lists = lists_all[0]
    value_lists = lists_all[1]
    key_count = key_lists.shape[3]
    block_ids = seq_index * blocks_local + jnp.arange(blocks_local)
    column_ids = jnp.arange(key_count)[None, :]
    middle_ok = jnp.where(
        (column_ids >= 2 * BLOCK) & (column_ids < 3 * BLOCK),
        (block_ids < total_blocks - 1)[:, None],
        True,
    )
    valid_mask = jnp.where(column_ids < BLOCK, (block_ids > 0)[:, None], middle_ok)
    query_blocks = to_blocks(query_rows)
    grad_blocks = to_blocks(grad_out)
    scores = (
        jnp.einsum("bhjqd,bhjkd->bhjqk", query_blocks, key_lists, preferred_element_type=f32)
        * score_scale
    )
    scores = jnp.where(valid_mask[None, None, :, None, :], scores, -1e30)
    row_max = jnp.max(scores, axis=-1, keepdims=True)
    log_total = row_max + jnp.log(jnp.sum(jnp.exp(scores - row_max), axis=-1, keepdims=True))
    weights = jnp.exp(scores - log_total)
    weights_b = weights.astype(bf16)
    mixed_rows = jnp.einsum(
        "bhjqk,bhjkd->bhjqd", weights_b, value_lists, preferred_element_type=f32
    )
    attended = from_blocks(mixed_rows.astype(bf16))
    row_delta = jnp.sum(grad_blocks.astype(f32) * mixed_rows, axis=-1, keepdims=True)
    grad_probs = jnp.einsum(
        "bhjqd,bhjkd->bhjqk", grad_blocks, value_lists, preferred_element_type=f32
    )
    dscore_b = (weights * (grad_probs - row_delta)).astype(bf16)
    grad_query = (
        jnp.einsum("bhjqk,bhjkd->bhjqd", dscore_b, key_lists, preferred_element_type=f32)
        * score_scale
    )

    def key_grads(lower, upper):
        key_part = (
            jnp.einsum(
                "bhjqk,bhjqd->bhjkd",
                dscore_b[..., lower:upper],
                query_blocks,
                preferred_element_type=f32,
            )
            * score_scale
        )
        value_part = jnp.einsum(
            "bhjqk,bhjqd->bhjkd",
            weights_b[..., lower:upper],
            grad_blocks,
            preferred_element_type=f32,
        )
        return jnp.stack([key_part, value_part])

    window_cols = 3 * BLOCK
    random_cols = pick_count * BLOCK
    window_grads = key_grads(0, window_cols).reshape(
        2, batch_count, heads_local, blocks_local, 3, BLOCK, head_dim
    )
    padded_grads = jnp.pad(
        window_grads[:, :, :, :, 0], ((0, 0), (0, 0), (0, 0), (0, 2), (0, 0), (0, 0))
    )
    padded_grads = padded_grads + jnp.pad(
        window_grads[:, :, :, :, 1], ((0, 0), (0, 0), (0, 0), (1, 1), (0, 0), (0, 0))
    )
    padded_grads = padded_grads + jnp.pad(
        window_grads[:, :, :, :, 2], ((0, 0), (0, 0), (0, 0), (2, 0), (0, 0), (0, 0))
    )
    own_grads = padded_grads[:, :, :, 1:-1]
    rim_grads = jnp.stack([padded_grads[:, :, :, 0], padded_grads[:, :, :, -1]], axis=3)
    returned = extended_2(rim_grads.astype(jnp.bfloat16), (("seq", 3),), 1).astype(rim_grads.dtype)
    own_grads = own_grads.at[:, :, :, 0].add(returned[:, :, :, 0])
    own_grads = own_grads.at[:, :, :, -1].add(returned[:, :, :, 3])
    global_grads = jnp.sum(key_grads(window_cols + random_cols, key_count), axis=3)
    global_grads = global_grads.transpose(0, 1, 3, 2, 4).reshape(
        2, batch_count, globals_count, columns
    )
    global_summed = global_sum(global_grads)
    inside = (local_pos >= 0) & (local_pos < tok_local)
    safe_pos = jnp.where(inside, local_pos, tok_local)
    global_local = (
        jnp.zeros((2, batch_count, tok_local, columns), f32)
        .at[:, :, safe_pos]
        .add(global_summed, mode="drop")
    )
    global_part = pair_blocks(global_local)
    target = ((which_batch * blocks_local + which_block) * heads_local + which_head).reshape(
        buffer_rows
    )
    random_grads = key_grads(window_cols, window_cols + random_cols)
    per_slot = random_grads.reshape(
        2, batch_count, heads_local, blocks_local, pick_count, BLOCK, head_dim
    )
    per_slot = per_slot.transpose(1, 2, 3, 4, 0, 5, 6).reshape(slot_count, 2, BLOCK, head_dim)
    sending = jnp.zeros((buffer_rows, 2, BLOCK, head_dim), f32).at[position].set(per_slot)
    arrived = lax.all_to_all(
        sending.astype(jnp.bfloat16), "seq", split_axis=0, concat_axis=0, tiled=True
    ).astype(sending.dtype)
    kept = jnp.where(slot_live[:, None, None, None], arrived, 0.0)
    summed = (
        jnp.zeros((batch_count * blocks_local * heads_local, 2, BLOCK, head_dim), f32)
        .at[target]
        .add(kept)
    )
    random_part = summed.reshape(
        batch_count, blocks_local, heads_local, 2, BLOCK, head_dim
    ).transpose(3, 0, 2, 1, 4, 5)
    total_grads = own_grads + random_part + global_part
    grad_key = from_blocks(total_grads[0].astype(bf16))
    grad_value = from_blocks(total_grads[1].astype(bf16))
    return (attended, from_blocks(grad_query.astype(bf16)), grad_key, grad_value)


def solution(mesh):
    return jax.shard_map(
        body,
        mesh=mesh,
        in_specs=(
            P(None, "seq", "head"),
            P(None, "seq", "head"),
            P(None, "seq", "head"),
            P(None, "seq", "head"),
            P(None, "head", None, None),
            P(),
        ),
        out_specs=(
            P(None, "seq", "head"),
            P(None, "seq", "head"),
            P(None, "seq", "head"),
            P(None, "seq", "head"),
        ),
        check_vma=False,
    )
```

profile of v0, /device:TPU:2, one launch (start us, length us, event | category | flops | bytes accessed | tf_op | source)
XLA Modules:
  0.0 617.9 jit_solution(17136765739606423861)
XLA Ops:
  12.8 2.2 gather_fusion
  15.0 12.2 %all-to-all-start = ((bf16[64,2,64,128]{3,2,1,0:T(8,128)(2,1)}), bf16[64,2,64,128]{3,2,1,0:T(8,128)(2,1)S(1)}, u32[]{:S(2)}, u32[]{:S(2)}) async-start(bf16[64,2,64,128]{3,2,1,0:T(8,128)(2,1)} %gather_fusion), calls=%async_computation | async-start | bytes 4194304 | tf_op jit(solution)/shard_map/all_to_all | solution.py:88
  28.4 4.3 collective-permute-start.1
  36.7 246.2 %all-reduce.7 = bf16[2,1,128,512]{2,3,0,1:T(8,128)(2,1)S(1)} all-reduce(f32[2,1,128,512]{2,3,0,1:T(8,128)} %convolution_bitcast_fusion.1), channel_id=1, replica_groups=mesh['seq'=64,'head'=4] {'seq'}, use_global_device_ids=true, to_apply=%region_4.5 | all-reduce | flops 131072 | bytes 786432 | tf_op jit(solution)/shard_map/psum | solution.py:52
  287.6 2.7 pad_maximum_fusion.2
  290.4 2.8 reshape.1153
  293.1 2.2 copy.122
  295.3 2.8 reshape.1152
  298.1 2.2 copy.118
  310.4 2.5 bitcast_reduce_fusion
  314.1 3.4 fusion.20
  317.4 2.5 fusion
  322.1 2.5 broadcast_in_dim.119
  324.6 7.8 %scatter_fusion = f32[64,2,64,128]{3,2,1,0:T(8,128)} fusion(f32[64,2,64,128]{3,2,1,0:T(8,128)} %broadcast_in_dim.119, s32[48]{0:T(128)S(1)} %fusion.62, f32[48,2,64,128]{3,2,1,0:T(8,128)S(1)} %bitcast.280), kind=kCustom, calls=%fused_computation.3 | custom fusion | bytes 9437376 | tf_op jit(solution)/shard_map/scatter | solution.py:202
  332.4 4.1 convert_element_type.125
  336.6 41.0 %all-to-all-start.1 = ((bf16[64,2,64,128]{3,2,1,0:T(8,128)(2,1)}), bf16[64,2,64,128]{3,2,1,0:T(8,128)(2,1)}, u32[]{:S(2)}, u32[]{:S(2)}) async-start(bf16[64,2,64,128]{3,2,1,0:T(8,128)(2,1)} %convert_element_type.125), calls=%async_computation.1 | async-start | bytes 4194304 | tf_op jit(solution)/shard_map/all_to_all | solution.py:203
  382.7 5.6 collective-permute-start.3
  391.4 2.8 fusion.12
  400.2 2.3 slice.213
  403.5 23.8 %collective-permute-done.2 = bf16[2,1,4,1,64,128]{5,4,0,2,3,1:T(8,128)(2,1)S(1)} collective-permute-done((bf16[2,1,4,1,64,128]{5,4,0,2,3,1:T(8,128)(2,1)}, bf16[2,1,4,1,64,128]{5,4,0,2,3,1:T(8,128)(2,1)S(1)}, u32[]{:S(2)}, u32[]{:S(2)}) %collective-permute-start.2) | collective-permute-done | bytes 131104 | tf_op jit(solution)/shard_map/ppermute | solution.py:16
  429.8 156.3 %all-reduce.6.cloned.1.call-done = f32[2,1,128,512]{2,3,0,1:T(8,128)} async-done(((f32[2,1,128,512]{2,3,0,1:T(8,128)}), f32[2,1,128,512]{2,3,0,1:T(8,128)}) %all-reduce.6.cloned.1.call-update) | async-done | bytes 524304 | tf_op jit(solution)/shard_map/psum | solution.py:52
  587.6 5.9 scatter_fusion.2
  594.5 3.9 convert_select_fusion
  598.5 8.8 %scatter_fusion.1 = f32[16,2,64,128]{3,2,1,0:T(8,128)S(1)} fusion(f32[16,2,64,128]{3,2,1,0:T(8,128)S(1)} %broadcast_in_dim.116, s32[64]{0:T(128)S(1)} %fusion.63, f32[64,2,64,128]{3,2,1,0:T(8,128)} %convert_select_fusion), kind=kCustom, calls=%fused_computation.4 | custom fusion | flops 1048576 | bytes 12583168 | tf_op jit(solution)/shard_map/scatter-add | solution.py:210
  (133 shorter events, 52.6 us)
Async XLA Ops:
  15.0 12.2 %copy-start.12 = (bf16[1,256,512]{2,1,0:T(8,128)(2,1)S(1)}, bf16[1,256,512]{2,1,0:T(8,128)(2,1)}, u32[]{:S(2)}) copy-start(bf16[1,256,512]{2,1,0:T(8,128)(2,1)} %param.11) | copy-start | bytes 786436
  15.0 12.3 %copy-start.13 = (bf16[1,256,512]{2,1,0:T(8,128)(2,1)S(1)}, bf16[1,256,512]{2,1,0:T(8,128)(2,1)}, u32[]{:S(2)}) copy-start(bf16[1,256,512]{2,1,0:T(8,128)(2,1)} %param.12) | copy-start | bytes 786436
  15.0 289.2 %all-to-all-start = ((bf16[64,2,64,128]{3,2,1,0:T(8,128)(2,1)}), bf16[64,2,64,128]{3,2,1,0:T(8,128)(2,1)S(1)}, u32[]{:S(2)}, u32[]{:S(2)}) async-start(bf16[64,2,64,128]{3,2,1,0:T(8,128)(2,1)} %gather_fusion), calls=%async_computation | async-start | bytes 4194304 | tf_op jit(solution)/shard_map/all_to_all | solution.py:88
  27.1 7.5 %copy-start.14 = (s32[1,4,256,3]{2,1,3,0:T(4,128)S(1)}, s32[1,4,256,3]{2,1,3,0:T(4,128)}, u32[]{:S(2)}) copy-start(s32[1,4,256,3]{2,1,3,0:T(4,128)} %param.14) | copy-start | bytes 36868
  27.2 8.1 %copy-start.15 = (s32[128]{0:T(128)S(1)}, s32[128]{0:T(128)}, u32[]{:S(2)}) copy-start(s32[128]{0:T(128)} %param.15) | copy-start | bytes 1540
  27.5 256.2 %copy-start.5 = (bf16[1,256,512]{1,2,0:T(8,128)(2,1)}, bf16[1,256,512]{1,2,0:T(8,128)(2,1)S(1)}, u32[]{:S(2)}) copy-start(bf16[1,256,512]{1,2,0:T(8,128)(2,1)S(1)} %copy.116) | copy-start | bytes 786436
  28.4 259.2 %collective-permute-start.1 = (bf16[2,1,64,512]{2,3,0,1:T(8,128)(2,1)}, bf16[2,1,64,512]{2,3,0,1:T(8,128)(2,1)}, u32[]{:S(2)}, u32[]{:S(2)}) collective-permute-start(bf16[2,1,64,512]{2,3,0,1:T(8,128)(2,1)} %get-tuple-element.41), channel_id=1, source_target_pairs={{4,0},{8,4},{12,8},{16,12},{20,16},{24,20},{28,24},{32,28},{36,32}... | collective-permute-start | bytes 393224 | tf_op jit(solution)/shard_map/ppermute | solution.py:17
  32.7 254.9 %collective-permute-start = (bf16[2,1,64,512]{2,3,0,1:T(8,128)(2,1)}, bf16[2,1,64,512]{2,3,0,1:T(8,128)(2,1)}, u32[]{:S(2)}, u32[]{:S(2)}) collective-permute-start(bf16[2,1,64,512]{2,3,0,1:T(8,128)(2,1)} %get-tuple-element.42), channel_id=1, source_target_pairs={{0,4},{4,8},{8,12},{12,16},{16,20},{20,24},{24,28},{28,32},{32,36}... | collective-permute-start | bytes 393224 | tf_op jit(solution)/shard_map/ppermute | solution.py:16
  285.7 34.2 %copy-start.2 = (bf16[1,4,64,4,128]{4,3,2,1,0:T(4,128)(2,1)}, bf16[1,4,64,4,128]{4,3,2,1,0:T(4,128)(2,1)S(1)}, u32[]{:S(2)}) copy-start(bf16[1,4,64,4,128]{4,3,2,1,0:T(4,128)(2,1)S(1)} %reshape.1078) | copy-start | bytes 786436
  300.2 3.0 copy-start.6
  307.7 1.4 copy-start.11
  314.1 6.6 %copy-start = (bf16[1,4,4,64,512]{4,3,2,1,0:T(8,128)(2,1)}, bf16[1,4,4,64,512]{4,3,2,1,0:T(8,128)(2,1)S(1)}, u32[]{:S(2)}) copy-start(bf16[1,4,4,64,512]{4,3,2,1,0:T(8,128)(2,1)S(1)} %fusion.25) | copy-start | bytes 3145732
  319.9 1.5 copy-start.7
  336.6 41.3 %copy-start.3 = (bf16[1,4,64,4,128]{4,3,2,1,0:T(4,128)(2,1)S(1)}, bf16[1,4,64,4,128]{4,3,2,1,0:T(4,128)(2,1)}, u32[]{:S(2)}) copy-start(bf16[1,4,64,4,128]{4,3,2,1,0:T(4,128)(2,1)} %copy-done.2) | copy-start | bytes 786436
  336.6 41.3 %copy-start.8 = (bf16[4,4,64,512]{3,2,1,0:T(8,128)(2,1)S(1)}, bf16[4,4,64,512]{3,2,1,0:T(8,128)(2,1)}, u32[]{:S(2)}) copy-start(bf16[4,4,64,512]{3,2,1,0:T(8,128)(2,1)} %copy-done.7) | copy-start | bytes 3145732
  336.6 258.0 %all-to-all-start.1 = ((bf16[64,2,64,128]{3,2,1,0:T(8,128)(2,1)}), bf16[64,2,64,128]{3,2,1,0:T(8,128)(2,1)}, u32[]{:S(2)}, u32[]{:S(2)}) async-start(bf16[64,2,64,128]{3,2,1,0:T(8,128)(2,1)} %convert_element_type.125), calls=%async_computation.1 | async-start | bytes 4194304 | tf_op jit(solution)/shard_map/all_to_all | solution.py:203
  377.5 1.2 copy-start.1
  377.6 208.5 %all-reduce.6.cloned.1.call-start = ((), (), s32[]{:S(2)}) async-start(), calls=%async_computation.2 | async-start | bytes 1048576 | tf_op jit(solution)/shard_map/psum | solution.py:52
  379.8 9.8 %copy-start.4 = (bf16[1,4,64,4,128]{4,3,2,1,0:T(4,128)(2,1)S(1)}, bf16[1,4,64,4,128]{4,3,2,1,0:T(4,128)(2,1)}, u32[]{:S(2)}) copy-start(bf16[1,4,64,4,128]{4,3,2,1,0:T(4,128)(2,1)} %copy-done.2) | copy-start | bytes 786436
  379.8 9.8 %copy-start.9 = (bf16[4,4,64,512]{3,2,1,0:T(8,128)(2,1)S(1)}, bf16[4,4,64,512]{3,2,1,0:T(8,128)(2,1)}, u32[]{:S(2)}) copy-start(bf16[4,4,64,512]{3,2,1,0:T(8,128)(2,1)} %copy-done.7) | copy-start | bytes 3145732
  380.6 46.7 %collective-permute-start.2 = (bf16[2,1,4,1,64,128]{5,4,0,2,3,1:T(8,128)(2,1)}, bf16[2,1,4,1,64,128]{5,4,0,2,3,1:T(8,128)(2,1)S(1)}, u32[]{:S(2)}, u32[]{:S(2)}) collective-permute-start(bf16[2,1,4,1,64,128]{5,4,0,2,3,1:T(8,128)(2,1)} %get-tuple-element.32), channel_id=1, source_target_pairs={{0,4},{4,8},{8,12},{12,16},{16,20},{20,24},{24,28},{28,32},{32,36}... | collective-permute-start | bytes 393224 | tf_op jit(solution)/shard_map/ppermute | solution.py:16
  382.7 44.6 %collective-permute-start.3 = (bf16[2,1,4,1,64,128]{5,4,0,2,3,1:T(8,128)(2,1)}, bf16[2,1,4,1,64,128]{5,4,0,2,3,1:T(8,128)(2,1)}, u32[]{:S(2)}, u32[]{:S(2)}) collective-permute-start(bf16[2,1,4,1,64,128]{5,4,0,2,3,1:T(8,128)(2,1)} %get-tuple-element.33), channel_id=1, source_target_pairs={{4,0},{8,4},{12,8},{16,12},{20,16},{24,20},{28,24},{32,28},{36,32}... | collective-permute-start | bytes 393224 | tf_op jit(solution)/shard_map/ppermute | solution.py:17
  394.2 0.9 copy-start.10
Sparse Core Ops, SparseCore 0:
  400.3 185.7 all-reduce.5
where the time goes:
time: 620 us; the launch traced here: 618 us
  blocking collectives  246 us (40%)
  waiting for transfers between devices  180 us (29%)
  starting transfers between devices  67.3 us (11%)
  local copies, waits for them, and re-layouts  55 us (9%)
  other arithmetic  38.2 us (6%)
  matrix products  16.3 us (3%)
  between operations  14.7 us (2%)
    psum x1, blocking collectives, global_sum(): return lax.psum(array, 'seq')  246 us
    psum x1, waiting for transfers between devices, global_sum(): return lax.psum(array, 'seq')  156 us
    all_to_all x1, starting transfers between devices, body(): lax.all_to_all(sending.astype(jnp.bfloat16), 'seq', split_axis=0, concat_...  41 us
    ppermute x2, waiting for transfers between devices, extended_2(): before = lax.ppermute(last, axis, up)  23.8 us
  transfers between devices with their start and end apart: 7, of which 2 were waited for; matrix products, arithmetic and copies ran while one was open for 9% of the time, Pallas kernels for 0%

commit v1 on v0

--- a/solution.py
+++ b/solution.py
@@ -49,7 +49,7 @@
         )
 
     def global_sum(array):
-        return lax.psum(array, "seq")
+        return jnp.sum(lax.all_gather(array, "seq"), axis=0)
 
     key_value = jnp.stack([key_rows, value_rows])
     edge_rows = jnp.concatenate([key_value[:, :, :BLOCK], key_value[:, :, -BLOCK:]], axis=2)

time: 620 us -> 423 us (0.68)
  blocking collectives: 246 us -> 0 us
  waiting for transfers between devices: 180 us -> 243 us
  starting transfers between devices: 67.3 us -> 32.5 us
  other arithmetic: 38.2 us -> 63.1 us
    psum x1 -> x0, blocking collectives: 246 us -> none  [global_sum(): return lax.psum(array, 'seq')]
    psum x1 -> x0, waiting for transfers between devices: 156 us -> none  [global_sum(): return lax.psum(array, 'seq')]
    all_gather x0 -> x2, waiting for transfers between devices: none -> 140 us  [global_sum(): return jnp.sum(lax.all_gather(array, 'seq'), axis=0)]
    ppermute x2, waiting for transfers between devices: 0.01 us -> 96.7 us  [extended_2(): after = lax.ppermute(first, axis, down)]
    all_to_all x1, starting transfers between devices: 41 us -> 7.88 us  [body(): lax.all_to_all(sending.astype(jnp.bfloat16), 'seq', split_axis=0, concat_...]
    reduce_sum x0 -> x2, other arithmetic: none -> 24.2 us  [global_sum(): return jnp.sum(lax.all_gather(array, 'seq'), axis=0)]
    ppermute x2, waiting for transfers between devices: 23.8 us -> 5.98 us  [extended_2(): before = lax.ppermute(last, axis, up)]
  transfers between devices with their start and end apart: 7 -> 8, of which waited for: 2 -> 6; matrix products, arithmetic and copies ran while one was open for 9% -> 18% of each run, Pallas kernels for 0% -> 0%
where the time goes in v1:
time: 423 us; the launch traced here: 420 us
  waiting for transfers between devices  243 us (57%)
  other arithmetic  63.1 us (15%)
  local copies, waits for them, and re-layouts  52.5 us (12%)
  starting transfers between devices  32.5 us (8%)
  between operations  14.7 us (3%)
  matrix products  14.6 us (3%)
    all_gather x2, waiting for transfers between devices, global_sum(): return jnp.sum(lax.all_gather(array, 'seq'), axis=0)  140 us
    ppermute x2, waiting for transfers between devices, extended_2(): after = lax.ppermute(first, axis, down)  96.7 us
    reduce_sum x2, other arithmetic, global_sum(): return jnp.sum(lax.all_gather(array, 'seq'), axis=0)  24.2 us
    all_to_all x1, starting transfers between devices, body(): lax.all_to_all(outgoing, 'seq', split_axis=0, concat_axis=0, tiled=True)  12 us
    reshape x5, local copies, waits for them, and re-layouts, pair_blocks(): array.reshape(2, batch_count, blocks_local, BLOCK, heads_local, head_dim)  10.9 us
    scatter-add x1, other arithmetic, body(): summed = jnp.zeros((batch_count * blocks_local * heads_local, 2, BLOCK, h...  9.03 us
    unnamed x39, local copies, waits for them, and re-layouts  8.81 us
    ppermute x2, starting transfers between devices, extended_2(): after = lax.ppermute(first, axis, down)  8.64 us
  transfers between devices with their start and end apart: 8, of which 6 were waited for; matrix products, arithmetic and copies ran while one was open for 18% of the time, Pallas kernels for 0%

profile of v1, /device:TPU:2, one launch (start us, length us, event | category | flops | bytes accessed | tf_op | source)
XLA Modules:
  0.0 420.3 jit_solution(8087833232464308902)
XLA Ops:
  16.8 12.0 %all-to-all-start = ((bf16[64,2,64,128]{3,2,1,0:T(8,128)(2,1)}), bf16[64,2,64,128]{3,2,1,0:T(8,128)(2,1)S(1)}, u32[]{:S(2)}, u32[]{:S(2)}) async-start(bf16[64,2,64,128]{3,2,1,0:T(8,128)(2,1)} %gather_fusion), calls=%async_computation | async-start | bytes 4194304 | tf_op jit(solution)/shard_map/all_to_all | solution.py:88
  29.8 4.3 %collective-permute-start.1 = (bf16[2,1,64,512]{2,3,0,1:T(8,128)(2,1)}, bf16[2,1,64,512]{2,3,0,1:T(8,128)(2,1)}, u32[]{:S(2)}, u32[]{:S(2)}) collective-permute-start(bf16[2,1,64,512]{2,3,0,1:T(8,128)(2,1)} %get-tuple-element.41), channel_id=1, source_target_pairs={{4,0},{8,4},{12,8},{16,12},{20,16},{24,20},{28,24},{32,28},{36,32}... | collective-permute-start | bytes 393224 | tf_op jit(solution)/shard_map/ppermute | solution.py:17
  39.0 57.1 %collective-permute-done.1 = bf16[2,1,64,512]{2,3,0,1:T(8,128)(2,1)} collective-permute-done((bf16[2,1,64,512]{2,3,0,1:T(8,128)(2,1)}, bf16[2,1,64,512]{2,3,0,1:T(8,128)(2,1)}, u32[]{:S(2)}, u32[]{:S(2)}) %collective-permute-start.1) | collective-permute-done | bytes 131104 | tf_op jit(solution)/shard_map/ppermute | solution.py:17
  96.1 3.6 collective-permute-done
  99.6 2.7 pad_maximum_fusion.2
  102.4 2.8 reshape.1167
  107.3 2.8 reshape.1168
  121.3 74.5 %all-gather.6.cloned.1.call-done = f32[128,1,128,512]{3,2,1,0:T(8,128)} async-done(((f32[2,1,128,512]{3,2,1,0:T(8,128)}), f32[128,1,128,512]{3,2,1,0:T(8,128)}) %all-gather.6.cloned.1.call-update) | async-done | bytes 33554448 | tf_op jit(solution)/shard_map/all_gather | solution.py:52
  195.8 12.1 %bitcast_reduce_fusion = bf16[2,128,512]{2,1,0:T(8,128)(2,1)S(1)} fusion(f32[64,2,128,512]{3,2,1,0:T(8,128)} %bitcast.275), kind=kLoop, calls=%fused_computation.6 | loop fusion | flops 8257536 | bytes 33816576 | tf_op jit(solution)/shard_map/reduce_sum | solution.py:52
  209.5 2.5 bitcast_reduce_fusion.1
  213.1 3.4 fusion.20
  216.5 2.5 fusion
  223.4 2.5 broadcast_in_dim.119
  225.9 8.0 %scatter_fusion = f32[64,2,64,128]{3,2,1,0:T(8,128)} fusion(f32[64,2,64,128]{3,2,1,0:T(8,128)} %broadcast_in_dim.119, s32[48]{0:T(128)S(1)} %fusion.62, f32[48,2,64,128]{3,2,1,0:T(8,128)S(1)} %bitcast.286), kind=kCustom, calls=%fused_computation.3 | custom fusion | bytes 9437376 | tf_op jit(solution)/shard_map/scatter | solution.py:202
  233.8 4.1 convert_element_type.138
  237.9 7.9 %all-to-all-start.1 = ((bf16[64,2,64,128]{3,2,1,0:T(8,128)(2,1)}), bf16[64,2,64,128]{3,2,1,0:T(8,128)(2,1)}, u32[]{:S(2)}, u32[]{:S(2)}) async-start(bf16[64,2,64,128]{3,2,1,0:T(8,128)(2,1)} %convert_element_type.138), calls=%async_computation.1 | async-start | bytes 4194304 | tf_op jit(solution)/shard_map/all_to_all | solution.py:203
  248.9 4.3 %collective-permute-start.3 = (bf16[2,1,4,1,64,128]{5,4,0,2,3,1:T(8,128)(2,1)}, bf16[2,1,4,1,64,128]{5,4,0,2,3,1:T(8,128)(2,1)S(1)}, u32[]{:S(2)}, u32[]{:S(2)}) collective-permute-start(bf16[2,1,4,1,64,128]{5,4,0,2,3,1:T(8,128)(2,1)} %get-tuple-element.33), channel_id=1, source_target_pairs={{4,0},{8,4},{12,8},{16,12},{20,16},{24,20},{28,24},{32,28},{36,32}... | collective-permute-start | bytes 393224 | tf_op jit(solution)/shard_map/ppermute | solution.py:17
  255.2 2.8 fusion.12
  265.7 39.6 %collective-permute-done.3 = bf16[2,1,4,1,64,128]{5,4,0,2,3,1:T(8,128)(2,1)S(1)} collective-permute-done((bf16[2,1,4,1,64,128]{5,4,0,2,3,1:T(8,128)(2,1)}, bf16[2,1,4,1,64,128]{5,4,0,2,3,1:T(8,128)(2,1)S(1)}, u32[]{:S(2)}, u32[]{:S(2)}) %collective-permute-start.3) | collective-permute-done | bytes 131104 | tf_op jit(solution)/shard_map/ppermute | solution.py:17
  311.0 4.1 convert_select_fusion
  315.3 9.0 %scatter_fusion.1 = f32[16,2,64,128]{3,2,1,0:T(8,128)S(1)} fusion(f32[16,2,64,128]{3,2,1,0:T(8,128)S(1)} %broadcast_in_dim.116, s32[64]{0:T(128)S(1)} %fusion.63, f32[64,2,64,128]{3,2,1,0:T(8,128)} %convert_select_fusion), kind=kCustom, calls=%fused_computation.4 | custom fusion | flops 1048576 | bytes 12583168 | tf_op jit(solution)/shard_map/scatter-add | solution.py:210
  324.3 65.8 %all-gather.4.cloned.1.call-done = f32[64,2,1,128,512]{4,3,2,1,0:T(8,128)} async-done(((f32[1,2,1,128,512]{4,3,2,1,0:T(8,128)}), f32[64,2,1,128,512]{4,3,2,1,0:T(8,128)}) %all-gather.4.cloned.1.call-update) | async-done | bytes 33554448 | tf_op jit(solution)/shard_map/all_gather | solution.py:52
  390.1 12.1 %reduce_sum.93 = f32[2,128,512]{2,1,0:T(8,128)S(1)} reduce(f32[64,2,1,128,512]{4,3,2,1,0:T(8,128)} %all-gather.4.cloned.1.call-done, f32[]{:T(128)} %constant.182.clone.1), dimensions={0,2}, to_apply=%region_12.13 | reduce | flops 8257536 | bytes 34078724 | tf_op jit(solution)/shard_map/reduce_sum | solution.py:52
  402.9 5.9 %scatter_fusion.2 = f32[2,256,512]{2,0,1:T(2,128)S(1)} fusion(f32[2,256,512]{2,0,1:T(2,128)S(1)} %broadcast.1025, s32[128]{0:T(128)S(1)} %get-tuple-element.30, f32[128,2,512]{2,1,0:T(2,128)S(1)} %copy.150), kind=kCustom, calls=%fused_computation.5 | custom fusion | flops 131072 | bytes 1573376 | tf_op jit(solution)/shard_map/scatter-add | solution.py:191
  (134 shorter events, 59.3 us)
Async XLA Ops:
  7.2 4.5 %copy-start.11 = (bf16[1,256,512]{2,1,0:T(8,128)(2,1)S(1)}, bf16[1,256,512]{2,1,0:T(8,128)(2,1)}, u32[]{:S(2)}) copy-start(bf16[1,256,512]{2,1,0:T(8,128)(2,1)} %param.11) | copy-start | bytes 786436
  7.2 188.6 %all-gather.6.cloned.1.call-start = ((), (), s32[]{:S(2)}) async-start(), calls=%async_computation.3 | async-start | bytes 34078720 | tf_op jit(solution)/shard_map/all_gather | solution.py:52
  7.2 4.5 %copy-start.12 = (bf16[1,256,512]{2,1,0:T(8,128)(2,1)S(1)}, bf16[1,256,512]{2,1,0:T(8,128)(2,1)}, u32[]{:S(2)}) copy-start(bf16[1,256,512]{2,1,0:T(8,128)(2,1)} %param.12) | copy-start | bytes 786436
  8.4 3.4 copy-start.13
  9.5 19.4 %copy-start.4 = (bf16[1,256,512]{1,2,0:T(8,128)(2,1)}, bf16[1,256,512]{1,2,0:T(8,128)(2,1)S(1)}, u32[]{:S(2)}) copy-start(bf16[1,256,512]{1,2,0:T(8,128)(2,1)S(1)} %copy.120) | copy-start | bytes 786436
  16.8 99.5 %all-to-all-start = ((bf16[64,2,64,128]{3,2,1,0:T(8,128)(2,1)}), bf16[64,2,64,128]{3,2,1,0:T(8,128)(2,1)S(1)}, u32[]{:S(2)}, u32[]{:S(2)}) async-start(bf16[64,2,64,128]{3,2,1,0:T(8,128)(2,1)} %gather_fusion), calls=%async_computation | async-start | bytes 4194304 | tf_op jit(solution)/shard_map/all_to_all | solution.py:88
  28.8 361.2 %all-gather.4.cloned.1.call-start = ((), (), s32[]{:S(2)}) async-start(), calls=%async_computation.2 | async-start | bytes 34078720 | tf_op jit(solution)/shard_map/all_gather | solution.py:52
  29.8 66.3 %collective-permute-start.1 = (bf16[2,1,64,512]{2,3,0,1:T(8,128)(2,1)}, bf16[2,1,64,512]{2,3,0,1:T(8,128)(2,1)}, u32[]{:S(2)}, u32[]{:S(2)}) collective-permute-start(bf16[2,1,64,512]{2,3,0,1:T(8,128)(2,1)} %get-tuple-element.41), channel_id=1, source_target_pairs={{4,0},{8,4},{12,8},{16,12},{20,16},{24,20},{28,24},{32,28},{36,32}... | collective-permute-start | bytes 393224 | tf_op jit(solution)/shard_map/ppermute | solution.py:17
  34.1 65.5 %collective-permute-start = (bf16[2,1,64,512]{2,3,0,1:T(8,128)(2,1)}, bf16[2,1,64,512]{2,3,0,1:T(8,128)(2,1)}, u32[]{:S(2)}, u32[]{:S(2)}) collective-permute-start(bf16[2,1,64,512]{2,3,0,1:T(8,128)(2,1)} %get-tuple-element.42), channel_id=1, source_target_pairs={{0,4},{4,8},{8,12},{12,16},{16,20},{20,24},{24,28},{28,32},{32,36}... | collective-permute-start | bytes 393224 | tf_op jit(solution)/shard_map/ppermute | solution.py:16
  38.9 183.1 %copy-start.2 = (bf16[1,4,64,4,128]{4,3,2,1,0:T(4,128)(2,1)}, bf16[1,4,64,4,128]{4,3,2,1,0:T(4,128)(2,1)S(1)}, u32[]{:S(2)}) copy-start(bf16[1,4,64,4,128]{4,3,2,1,0:T(4,128)(2,1)S(1)} %reshape.1091) | copy-start | bytes 786436
  112.3 3.1 copy-start.5
  213.1 8.1 %copy-start = (bf16[1,4,4,64,512]{4,3,2,1,0:T(8,128)(2,1)}, bf16[1,4,4,64,512]{4,3,2,1,0:T(8,128)(2,1)S(1)}, u32[]{:S(2)}) copy-start(bf16[1,4,4,64,512]{4,3,2,1,0:T(8,128)(2,1)S(1)} %fusion.25) | copy-start | bytes 3145732
  219.0 1.0 copy-start.6
  220.2 1.8 copy-start.7
  237.9 7.9 %copy-start.3 = (bf16[1,4,64,4,128]{4,3,2,1,0:T(4,128)(2,1)S(1)}, bf16[1,4,64,4,128]{4,3,2,1,0:T(4,128)(2,1)}, u32[]{:S(2)}) copy-start(bf16[1,4,64,4,128]{4,3,2,1,0:T(4,128)(2,1)} %copy-done.2) | copy-start | bytes 786436
  237.9 8.0 %copy-start.8 = (bf16[4,4,64,512]{3,2,1,0:T(8,128)(2,1)S(1)}, bf16[4,4,64,512]{3,2,1,0:T(8,128)(2,1)}, u32[]{:S(2)}) copy-start(bf16[4,4,64,512]{3,2,1,0:T(8,128)(2,1)} %copy-done.6) | copy-start | bytes 3145732
  237.9 73.1 %all-to-all-start.1 = ((bf16[64,2,64,128]{3,2,1,0:T(8,128)(2,1)}), bf16[64,2,64,128]{3,2,1,0:T(8,128)(2,1)}, u32[]{:S(2)}, u32[]{:S(2)}) async-start(bf16[64,2,64,128]{3,2,1,0:T(8,128)(2,1)} %convert_element_type.138), calls=%async_computation.1 | async-start | bytes 4194304 | tf_op jit(solution)/shard_map/all_to_all | solution.py:203
  245.8 1.2 copy-start.1
  248.1 7.0 %copy-start.9 = (bf16[4,4,64,512]{3,2,1,0:T(8,128)(2,1)S(1)}, bf16[4,4,64,512]{3,2,1,0:T(8,128)(2,1)}, u32[]{:S(2)}) copy-start(bf16[4,4,64,512]{3,2,1,0:T(8,128)(2,1)} %copy-done.6) | copy-start | bytes 3145732
  248.9 56.4 %collective-permute-start.3 = (bf16[2,1,4,1,64,128]{5,4,0,2,3,1:T(8,128)(2,1)}, bf16[2,1,4,1,64,128]{5,4,0,2,3,1:T(8,128)(2,1)S(1)}, u32[]{:S(2)}, u32[]{:S(2)}) collective-permute-start(bf16[2,1,4,1,64,128]{5,4,0,2,3,1:T(8,128)(2,1)} %get-tuple-element.33), channel_id=1, source_target_pairs={{4,0},{8,4},{12,8},{16,12},{20,16},{24,20},{28,24},{32,28},{36,32}... | collective-permute-start | bytes 393224 | tf_op jit(solution)/shard_map/ppermute | solution.py:17
  253.2 54.4 %collective-permute-start.2 = (bf16[2,1,4,1,64,128]{5,4,0,2,3,1:T(8,128)(2,1)}, bf16[2,1,4,1,64,128]{5,4,0,2,3,1:T(8,128)(2,1)}, u32[]{:S(2)}, u32[]{:S(2)}) collective-permute-start(bf16[2,1,4,1,64,128]{5,4,0,2,3,1:T(8,128)(2,1)} %get-tuple-element.32), channel_id=1, source_target_pairs={{0,4},{4,8},{8,12},{12,16},{16,20},{20,24},{24,28},{28,32},{32,36}... | collective-permute-start | bytes 393224 | tf_op jit(solution)/shard_map/ppermute | solution.py:16
  258.0 1.4 copy-start.10
Sparse Core Ops, SparseCore 0:
  11.7 183.9 all-gather.5
  221.4 168.6 all-gather.3
